TPU v7x, 32 devices: a whole 2x2x4 slice. The times are simulated.
32 devices in a mesh: row: 8 (over z, y), col: 4 (over x, core).
Axes of the slice: x: 2, y: 2, z: 4, core: 2. Of those that a mesh axis runs over, the one named last changes fastest.
Arguments:
- matrix_blocks: bfloat16 [16, 24, 256, 256], P('row', 'col'), may hold values from 0 to 10, as said below
- matrix_rows: int32 [16, 24], P('row', 'col'), may hold values from 0 to 7, as said below
- matrix_counts: int32 [16, 4], P('row', 'col'), may hold values from 0 to 6, as said below
- slab_blocks: bfloat16 [16, 16, 256, 256], P('row', 'col'), may hold values from 0.099609375 to 1
- slab_inner: int32 [16, 16], P('row', 'col'), may hold values from 0 to 15, as said below
- slab_counts: int32 [16], P('row'), may hold values from 8 to 16
Outputs:
- inflated: bfloat16 [16, 32, 256, 256], P('row', 'col')
Inputs may be any that keep to these rules, and one draw needn't show every extreme that they name: `matrix_blocks`: entries are positive. `matrix_rows`: the 6 slots of one matrix block column within one index of col name distinct block rows. `matrix_counts`: each row sums to 16; every matrix block column has an index of col where all 6 slots are live. `slab_inner`: the 16 entries of a row are distinct.
All inputs are finite; a program needn't handle non-finite values.
Results may differ from a plain program's by a relative error of at most 0.001.
Values may be sent and summed in bfloat16 or wider, within the bound.
A program may use at most 192 MiB of HBM per device.

v0:
```python
import jax
import jax.numpy as jnp
from jax import lax
from jax.sharding import PartitionSpec as P

RB_DEV = 8


HIGHEST = lax.Precision.HIGHEST


def on_device(matrix_blocks, matrix_rows, matrix_counts, slab_blocks, slab_inner, slab_counts):
    capacity = matrix_rows.shape[1]
    columns = slab_blocks.shape[0]
    block = slab_blocks.shape[2]
    window_index = jnp.arange(RB_DEV, dtype=jnp.int32)
    slot_index = jnp.arange(capacity, dtype=jnp.int32)
    initial = jnp.zeros((columns, RB_DEV, block, block), jnp.float32)
    whole_blocks, whole_rows, whole_counts = (
        lax.all_gather(matrix_blocks, "row", axis=0, tiled=True),
        lax.all_gather(matrix_rows, "row", axis=0, tiled=True),
        lax.all_gather(matrix_counts, "row", axis=0, tiled=True),
    )
    part_blocks = lax.all_gather(slab_blocks, "col", axis=1, tiled=True)
    part_inner = lax.all_gather(slab_inner, "col", axis=1, tiled=True)
    breadth = part_inner.shape[1]
    live = jnp.arange(breadth, dtype=jnp.int32)[None, :] < slab_counts[:, None]
    selected = whole_blocks[part_inner]
    chosen_rows = whole_rows[part_inner]
    chosen_counts = whole_counts[part_inner, 0]
    active = (slot_index < chosen_counts[..., None]) & live[..., None]
    weight = ((chosen_rows[..., None] == window_index) & active[..., None]).astype(jnp.float32)
    products = jnp.einsum(
        "jqtxz,jqzy->jqtxy", selected, part_blocks, preferred_element_type=jnp.float32
    )
    expanded = initial + jnp.einsum("jqti,jqtxy->jixy", weight, products, precision=HIGHEST)
    squared = expanded * expanded
    local_sums = jnp.sum(squared, axis=(1, 2))
    total_rows = float(RB_DEV * lax.axis_size("col") * block)
    sums = lax.psum(local_sums, "col")
    factor = total_rows / sums
    return (squared * factor[:, None, None, :]).astype(jnp.bfloat16)


def solution(mesh):
    return jax.shard_map(
        on_device,
        mesh=mesh,
        in_specs=(
            P("row", "col", None, None),
            P("row", "col"),
            P("row", "col"),
            P("row", "col", None, None),
            P("row", "col"),
            P("row"),
        ),
        out_specs=P("row", "col", None, None),
        check_vma=False,
    )
```

profile of v0, /device:TPU:0, one launch (start us, length us, event | category | flops | bytes accessed | tf_op | source)
XLA Modules:
  0.0 324.3 jit_solution(4459497595355420207)
XLA Ops:
  6.5 0.0 all-gather.5.cloned.1.call-start
  6.5 0.7 all-gather.5.cloned.1.call-update
  7.3 0.0 all-gather.7.cloned.1.call-start
  7.3 0.7 all-gather.7.cloned.1.call-update
  8.0 1.2 dynamic-slice
  9.9 0.8 bitcast_dynamic-update-slice_fusion
  10.7 13.1 %all-reduce.1 = s32[16]{0:T(128)S(1)} all-reduce(s32[16]{0:T(128)S(1)} %bitcast_dynamic-update-slice_fusion), channel_id=1, replica_groups=mesh['row'=8,'col'=4] {'row'}, use_global_device_ids=true, to_apply=%add.1 | all-reduce | flops 16 | bytes 128
  23.7 5.3 %all-gather.1 = s32[4,4,2]{1,2,0:T(2,128)S(1)} all-gather(s32[1,4,2]{1,2,0:T(2,128)} %bitcast.41), channel_id=1, replica_groups=mesh['row'=8,'col'=4] {'col'}, dimensions={0}, use_global_device_ids=true | all-gather | bytes 160 | tf_op jit(solution)/shard_map/all_gather | solution.py:25
  29.0 0.1 reshape.66
  29.1 0.1 reshape.30
  29.2 18.3 %all-gather = s32[8,2,6]{2,1,0:T(2,128)S(1)} all-gather(s32[1,2,6]{2,1,0:T(2,128)} %bitcast.42), channel_id=1, replica_groups=mesh['row'=8,'col'=4] {'row'}, dimensions={0}, use_global_device_ids=true | all-gather | bytes 432 | tf_op jit(solution)/shard_map/all_gather | solution.py:21
  47.5 0.6 gather_fusion
  48.1 0.1 copy.14
  48.1 0.1 reshape.36
  48.2 0.7 gather_fusion.1
  48.9 0.1 reshape.39
  49.0 0.7 iota_compare_fusion.2
  49.8 138.9 %all-gather.5.cloned.1.call-done = bf16[16,6,256,256]{3,2,1,0:T(8,128)(2,1)} async-done(((bf16[2,6,256,256]{3,2,1,0:T(8,128)(2,1)}), bf16[16,6,256,256]{3,2,1,0:T(8,128)(2,1)}) %all-gather.5.cloned.1.call-update) | async-done | bytes 12582928 | tf_op jit(solution)/shard_map/all_gather | solution.py:20
  188.7 15.3 %gather_fusion.2 = bf16[32,6,256,256]{3,2,1,0:T(8,128)(2,1)} fusion(bf16[16,6,256,256]{3,2,1,0:T(8,128)(2,1)} %all-gather.5.cloned.1.call-done, s32[1024]{0:T(1024)S(1)} %pad_clamp_fusion), kind=kCustom, calls=%fused_computation.2 | custom fusion | bytes 50331776 | tf_op jit(solution)/shard_map/gather | solution.py:28
  204.0 19.0 %all-gather.7.cloned.1.call-done = bf16[2,16,256,256]{3,2,1,0:T(8,128)(2,1)} async-done(((bf16[2,4,256,256]{3,2,1,0:T(8,128)(2,1)}), bf16[2,16,256,256]{3,2,1,0:T(8,128)(2,1)}) %all-gather.7.cloned.1.call-update) | async-done | bytes 4194320 | tf_op jit(solution)/shard_map/all_gather | solution.py:24
  222.9 25.9 %fusion.2 = f32[2,16,6,256,256]{4,3,2,1,0:T(8,128)} fusion(bf16[2,16,6,256,256]{4,3,2,1,0:T(8,128)(2,1)} %bitcast.38, bf16[2,16,256,256]{3,2,1,0:T(8,128)(2,1)} %all-gather.7.cloned.1.call-done), kind=kOutput, calls=%fused_computation.5 | convolution fusion | flops 6442450944 | bytes 79691776 | tf_op jit(solution)/shard_map/jqtxz,jqzy->jqtxy/dot_general | solution.py:33
  248.9 58.3 %fusion.4 = (f32[2,256]{1,0:T(2,128)S(1)}, f32[2,8,256,256,1]{3,1,4,2,0:T(8,128)}) fusion(f32[2,16,6,256,256]{4,3,2,1,0:T(8,128)} %fusion.2, s32[2,16,6]{1,2,0:T(8,128)S(1)} %copy.14, pred[2,16,6]{1,2,0:T(8,128)(4,1)S(1)} %fusion.10), kind=kOutput, calls=%fused_computation.9 | convolution fusion | flops 1210059264 | bytes 54528960 | tf_op jit(solution)/shard_map/jqti,jqtxy->jixy/dot_general | solution.py:36
  307.2 5.9 %psum.7 = f32[2,256]{1,0:T(2,128)S(1)} all-reduce(f32[2,256]{1,0:T(2,128)S(1)} %get-tuple-element.7), channel_id=1, replica_groups=mesh['row'=8,'col'=4] {'col'}, use_global_device_ids=true, to_apply=%region_1.0 | all-reduce | flops 512 | bytes 4096 | tf_op jit(solution)/shard_map/psum | solution.py:40
  313.1 2.6 multiply_convert_fusion
  315.7 1.8 copy.16
  (6 shorter events, 0.0 us)
Async XLA Ops:
  6.5 182.1 %all-gather.5.cloned.1.call-start = ((), (), s32[]{:S(2)}) async-start(), calls=%async_computation | async-start | bytes 14155776 | tf_op jit(solution)/shard_map/all_gather | solution.py:20
  7.3 215.7 %all-gather.7.cloned.1.call-start = ((), (), s32[]{:S(2)}) async-start(), calls=%async_computation.1 | async-start | bytes 5242880 | tf_op jit(solution)/shard_map/all_gather | solution.py:24
Sparse Core Ops, SparseCore 0:
  9.5 179.0 all-gather.4
  190.2 32.6 all-gather.6
where the time goes:
time: 325 us; the launch traced here: 324 us
  waiting for transfers between devices  159 us (49%)
  matrix products  84.3 us (26%)
  blocking collectives  42.5 us (13%)
  local copies, waits for them, and re-layouts  20.8 us (6%)
  between operations  14.1 us (4%)
  other arithmetic  3.36 us (1%)
    all_gather x1, waiting for transfers between devices, on_device(): lax.all_gather(matrix_blocks, 'row', axis=0, tiled=True)  139 us
    dot_general x1, matrix products, on_device(): jnp.einsum('jqti,jqtxy->jixy', weight, products, precision=HIGHEST)  58.3 us
    dot_general x1, matrix products, on_device(): jnp.einsum('jqtxz,jqzy->jqtxy', selected, part_blocks, preferred_element_...  25.9 us
    all_gather x1, waiting for transfers between devices, on_device(): part_blocks = lax.all_gather(slab_blocks, 'col', axis=1, tiled=True)  19 us
    all_gather x1, blocking collectives, on_device(): lax.all_gather(matrix_rows, 'row', axis=0, tiled=True)  18.3 us
    gather x1, local copies, waits for them, and re-layouts, on_device(): selected = whole_blocks[part_inner]  15.3 us
    unnamed x1, blocking collectives  13.1 us
  transfers between devices with their start and end apart: 2, of which 2 were waited for; matrix products, arithmetic and copies ran while one was open for 6% of the time, Pallas kernels for 0%

commit v1 on v0

v1 whole, which is shorter than its diff:
```python
import functools

import jax
import jax.numpy as jnp
from jax import lax
from jax.experimental import pallas as pl
from jax.experimental.pallas import tpu as pltpu
from jax.sharding import PartitionSpec as P

RB_DEV = 8
MESH = pl.DeviceIdType.MESH
CHUNKS = 6
PLAIN = CHUNKS - 1
UP, DOWN, SIDE = 0, 1, 2


def gather_kernel(n_row, n_col, a_ref, b_ref, mr_ref, mc_ref, a_all, b_all, mr_all, mc_all,
                  send, recv, b_send, b_recv, mr_send, mr_recv, mc_send, mc_recv, local):
    n_z = n_row // 2
    r = lax.axis_index("row")
    c = lax.axis_index("col")
    z = lax.div(r, 2)
    y = lax.rem(r, 2)
    other = 1 - y

    barrier = pltpu.get_barrier_semaphore()
    for d in range(1, n_row):
        pl.semaphore_signal(barrier, inc=1, device_id={"row": lax.rem(r + d, n_row)}, device_id_type=MESH)
    for d in range(1, n_col):
        pl.semaphore_signal(barrier, inc=1, device_id={"col": lax.rem(c + d, n_col)}, device_id_type=MESH)
    pl.semaphore_wait(barrier, n_row + n_col - 2)

    def chunk(way, rank, ch, own=False):
        target = {UP: r + 2, DOWN: r - 2, SIDE: 2 * z + other}[way]
        src = a_ref.at[ch] if own else a_all.at[rank, ch]
        return pltpu.make_async_remote_copy(
            src_ref=src, dst_ref=a_all.at[rank, ch], send_sem=send.at[way, rank, ch],
            recv_sem=recv.at[rank, ch], device_id={"row": target}, device_id_type=MESH)

    def arrived(rank, ch):
        pltpu.make_async_remote_copy(
            src_ref=a_all.at[rank, ch], dst_ref=a_all.at[rank, ch], send_sem=send.at[SIDE, rank, ch],
            recv_sem=recv.at[rank, ch], device_id={"row": 2 * z + other}, device_id_type=MESH).wait_recv()

    has_up = z < n_z - 1
    has_down = z > 0

    def small(d):
        return pltpu.make_async_remote_copy(
            src_ref=mr_ref, dst_ref=mr_all.at[r], send_sem=mr_send.at[d], recv_sem=mr_recv.at[d],
            device_id={"row": lax.rem(r + d, n_row)}, device_id_type=MESH)

    def slab(d):
        target = {"col": lax.rem(c + d, n_col)}
        return (
            pltpu.make_async_remote_copy(
                src_ref=mc_ref, dst_ref=mc_all.at[c], send_sem=mc_send.at[d], recv_sem=mc_recv.at[d],
                device_id=target, device_id_type=MESH),
            pltpu.make_async_remote_copy(
                src_ref=b_ref, dst_ref=b_all.at[c], send_sem=b_send.at[d], recv_sem=b_recv.at[d],
                device_id=target, device_id_type=MESH),
        )

    for ch in [PLAIN] + list(range(PLAIN)):
        chunk(SIDE, r, ch, True).start()
    for ch in range(CHUNKS):
        @pl.when(has_up)
        def _():
            chunk(UP, r, ch, True).start()

        @pl.when(has_down)
        def _():
            chunk(DOWN, r, ch, True).start()

    for d in range(1, n_row):
        small(d).start()
    for d in range(1, n_col):
        for copy in slab(d):
            copy.start()
    mine = (
        pltpu.make_async_copy(a_ref, a_all.at[r], local.at[0]),
        pltpu.make_async_copy(b_ref, b_all.at[c], local.at[1]),
        pltpu.make_async_copy(mr_ref, mr_all.at[r], local.at[2]),
        pltpu.make_async_copy(mc_ref, mc_all.at[c], local.at[3]),
    )
    for copy in mine:
        copy.start()

    beside = 2 * z + other
    arrived(beside, PLAIN)

    @pl.when(has_up)
    def _():
        chunk(UP, beside, PLAIN).start()

    @pl.when(has_down)
    def _():
        chunk(DOWN, beside, PLAIN).start()

    steps = [(0, ch, True) for ch in range(PLAIN)] + [(0, PLAIN, False), (1, PLAIN, False)]

    def relay(d, carry):
        for flip, ch, cross in steps:
            column = other if flip else y

            @pl.when(z >= d)
            def _():
                rank = 2 * (z - d) + column
                arrived(rank, ch)

                @pl.when(has_up)
                def _():
                    chunk(UP, rank, ch).start()

                if cross:
                    chunk(SIDE, rank, ch).start()

            @pl.when(z + d < n_z)
            def _():
                rank = 2 * (z + d) + column
                arrived(rank, ch)

                @pl.when(has_down)
                def _():
                    chunk(DOWN, rank, ch).start()

                if cross:
                    chunk(SIDE, rank, ch).start()
        return carry

    lax.fori_loop(1, n_z, relay, 0)

    def crossed(q, carry):
        for ch in range(PLAIN):
            arrived(2 * q + other, ch)
        return carry

    lax.fori_loop(0, n_z, crossed, 0)

    for copy in mine:
        copy.wait()
    for d in range(1, n_row):
        small(d).wait()
    for d in range(1, n_col):
        for copy in slab(d):
            copy.wait()

    for ch in range(CHUNKS):
        chunk(SIDE, r, ch, True).wait_send()

        @pl.when(has_up)
        def _():
            chunk(UP, r, ch, True).wait_send()

        @pl.when(has_down)
        def _():
            chunk(DOWN, r, ch, True).wait_send()

    @pl.when(has_up)
    def _():
        chunk(UP, beside, PLAIN).wait_send()

    @pl.when(has_down)
    def _():
        chunk(DOWN, beside, PLAIN).wait_send()

    def drain(d, carry):
        for flip, ch, cross in steps:
            column = other if flip else y

            @pl.when(z >= d)
            def _():
                rank = 2 * (z - d) + column

                @pl.when(has_up)
                def _():
                    chunk(UP, rank, ch).wait_send()

                if cross:
                    chunk(SIDE, rank, ch).wait_send()

            @pl.when(z + d < n_z)
            def _():
                rank = 2 * (z + d) + column

                @pl.when(has_down)
                def _():
                    chunk(DOWN, rank, ch).wait_send()

                if cross:
                    chunk(SIDE, rank, ch).wait_send()
        return carry

    lax.fori_loop(1, n_z, drain, 0)


def product_kernel(columns, capacity, slots, n_col, mr, mc, counts, a_ref, b_ref, sq_ref, sums_ref, where):
    step = pl.program_id(0)
    last = pl.num_programs(0) - 1
    per_rank = a_ref.shape[1] // capacity
    n_k = where.shape[1]

    @pl.when(step == 0)
    def _():
        sq_ref[...] = jnp.zeros_like(sq_ref)
        for j in range(columns):
            def clear(k, carry):
                where[j, k] = -1
                return carry

            lax.fori_loop(0, n_k, clear, 0)

            def place(q, carry):
                where[j, mc[lax.div(q, slots), 0, j * slots + lax.rem(q, slots)]] = q
                return carry

            lax.fori_loop(0, counts[j], place, 0)

    for kk in range(per_rank):
        live = mr[step, 1, kk]
        for j in range(columns):
            q = where[j, step * per_rank + kk]

            @pl.when(q >= 0)
            def _():
                right = b_ref[lax.div(q, slots), j * slots + lax.rem(q, slots)]

                def multiply(t, carry):
                    i = mr[step, 0, kk * capacity + t]
                    sq_ref[j, i] += jnp.dot(a_ref[0, kk * capacity + t], right,
                                            preferred_element_type=jnp.float32)
                    return carry

                lax.fori_loop(0, live, multiply, 0)

    @pl.when(step == last)
    def _():
        block = sq_ref.shape[2]
        for j in range(columns):
            def square(i, total):
                value = sq_ref[j, i]
                value = value * value
                sq_ref[j, i] = value
                return total + jnp.sum(value.reshape(block // 8, 8, block), axis=0)

            total = lax.fori_loop(0, RB_DEV, square, jnp.zeros((8, block), jnp.float32))
            sums_ref[j] = total


def on_device(n_row, n_col, matrix_blocks, matrix_rows, matrix_counts, slab_blocks, slab_inner, slab_counts):
    per_rank, capacity, block = matrix_blocks.shape[0], matrix_blocks.shape[1], matrix_blocks.shape[2]
    columns, slots = slab_blocks.shape[0], slab_blocks.shape[1]
    held = per_rank * capacity
    size = held // CHUNKS
    a = matrix_blocks.reshape(CHUNKS, size, block, block)
    b = slab_blocks.reshape(columns * slots, block, block)
    mr = jnp.zeros((8, 128), jnp.int32)
    mr = mr.at[0, :held].set(matrix_rows.reshape(held)).at[1, :per_rank].set(matrix_counts.reshape(per_rank))
    mc = jnp.zeros((8, 128), jnp.int32).at[0, :columns * slots].set(slab_inner.reshape(columns * slots))

    hbm = pl.BlockSpec(memory_space=pl.ANY)
    dma = pltpu.SemaphoreType.DMA
    a_all, b_all, mr_all, mc_all = pl.pallas_call(
        functools.partial(gather_kernel, n_row, n_col),
        out_shape=(
            jax.ShapeDtypeStruct((n_row,) + a.shape, a.dtype),
            jax.ShapeDtypeStruct((n_col,) + b.shape, b.dtype),
            jax.ShapeDtypeStruct((n_row, 8, 128), jnp.int32),
            jax.ShapeDtypeStruct((n_col, 8, 128), jnp.int32),
        ),
        in_specs=[hbm] * 4,
        out_specs=(hbm,) * 4,
        scratch_shapes=[
            dma((3, n_row, CHUNKS)), dma((n_row, CHUNKS)),
            dma((n_col,)), dma((n_col,)), dma((n_row,)), dma((n_row,)), dma((n_col,)), dma((n_col,)),
            dma((4,)),
        ],
        compiler_params=pltpu.CompilerParams(collective_id=0, has_side_effects=True),
        name="gather_blocks",
    )(a, b, mr, mc)
    a_all = a_all.reshape(n_row, held, block, block)

    squared, partial = pl.pallas_call(
        functools.partial(product_kernel, columns, capacity, slots, n_col),
        out_shape=(
            jax.ShapeDtypeStruct((columns, RB_DEV, block, block), jnp.float32),
            jax.ShapeDtypeStruct((columns, 8, block), jnp.float32),
        ),
        grid_spec=pltpu.PrefetchScalarGridSpec(
            num_scalar_prefetch=3,
            grid=(n_row,),
            in_specs=[
                pl.BlockSpec((1, held, block, block), lambda s, *_: (s, 0, 0, 0)),
                pl.BlockSpec((n_col, columns * slots, block, block), lambda s, *_: (0, 0, 0, 0)),
            ],
            out_specs=(
                pl.BlockSpec((columns, RB_DEV, block, block), lambda s, *_: (0, 0, 0, 0)),
                pl.BlockSpec((columns, 8, block), lambda s, *_: (0, 0, 0)),
            ),
            scratch_shapes=[pltpu.SMEM((columns, n_row * per_rank), jnp.int32)],
        ),
        compiler_params=pltpu.CompilerParams(vmem_limit_bytes=40 << 20),
        name="block_products",
    )(mr_all, mc_all, slab_counts, a_all, b_all)
    total_rows = float(RB_DEV * n_col * block)
    sums = lax.psum(jnp.sum(partial, axis=1), "col")
    factor = total_rows / sums
    return (squared * factor[:, None, None, :]).astype(jnp.bfloat16)


def solution(mesh):
    return jax.shard_map(
        functools.partial(on_device, mesh.shape["row"], mesh.shape["col"]),
        mesh=mesh,
        in_specs=(
            P("row", "col", None, None),
            P("row", "col"),
            P("row", "col"),
            P("row", "col", None, None),
            P("row", "col"),
            P("row"),
        ),
        out_specs=P("row", "col", None, None),
        check_vma=False,
    )
```

time: 325 us -> 175 us (0.54)
  waiting for transfers between devices: 159 us -> 0 us
  Pallas kernels: 0 us -> 153 us
  matrix products: 84.3 us -> 0 us
  blocking collectives: 42.5 us -> 8.38 us
  between operations: 14.1 us -> 0.05 us
  local copies, waits for them, and re-layouts: 20.8 us -> 9.69 us
    all_gather x2 -> x0, waiting for transfers between devices: 158 us -> none  [the longest x1 139 us: on_device(): lax.all_gather(matrix_blocks, 'row', axis=0, tiled=True)]
    pallas_call x0 -> x2, Pallas kernels: none -> 153 us  [the longest x1 128 us: on_device(): pl.pallas_call(functools.partial(gather_kernel, n_row, n_col), out_shape=...]
    dot_general x2 -> x0, matrix products: 84.3 us -> none  [the longest x1 58.3 us: on_device(): jnp.einsum('jqti,jqtxy->jixy', weight, products, precision=HIGHEST)]
    all_gather x2 -> x0, blocking collectives: 23.6 us -> none  [the longest x1 18.3 us: on_device(): lax.all_gather(matrix_rows, 'row', axis=0, tiled=True)]
    gather x5 -> x0, local copies, waits for them, and re-layouts: 16.7 us -> none  [the longest x1 15.3 us: on_device(): selected = whole_blocks[part_inner]]
    unnamed x1 -> x0, blocking collectives: 13.1 us -> none
    unnamed x4 -> x12, local copies, waits for them, and re-layouts: 2.08 us -> 6.82 us
  transfers between devices with their start and end apart: 2 -> 0, of which waited for: 2 -> 0; matrix products, arithmetic and copies ran while one was open for 6% -> 0% of each run, Pallas kernels for 0% -> 0%
where the time goes in v1:
time: 175 us
  Pallas kernels  153 us (87%)
  local copies, waits for them, and re-layouts  9.69 us (6%)
  blocking collectives  8.38 us (5%)
  other arithmetic  3.97 us (2%)
    pallas_call x1, Pallas kernels, on_device(): pl.pallas_call(functools.partial(gather_kernel, n_row, n_col), out_shape=...  128 us
    pallas_call x1, Pallas kernels, on_device(): pl.pallas_call(functools.partial(product_kernel, columns, capacity, slots...  25 us
    psum x1, blocking collectives, on_device(): sums = lax.psum(jnp.sum(partial, axis=1), 'col')  8.38 us
    unnamed x12, local copies, waits for them, and re-layouts  6.82 us
    convert_element_type x1, other arithmetic, on_device(): return (squared * factor[:, None, None, :]).astype(jnp.bfloat16)  3.94 us

profile of v1, /device:TPU:0, one launch (start us, length us, event | category | flops | bytes accessed | tf_op | source)
XLA Modules:
  0.0 175.2 jit_solution(7088406173014113815)
XLA Ops:
  0.0 0.8 reshape.104
  0.8 0.8 reshape.106
  1.5 0.6 scatter.14.mc_ref
  2.1 0.7 scatter.11.mr_ref
  2.9 0.0 copy-start.5
  2.9 0.6 copy-done.5
  3.5 128.1 %gather_blocks.1 = (bf16[8,6,2,256,256]{4,3,2,1,0:T(8,128)(2,1)}, bf16[4,8,256,256]{3,2,1,0:T(8,128)(2,1)}, s32[8,8,128]{2,1,0:T(8,128)}, s32[4,8,128]{2,1,0:T(8,128)}) custom-call(bf16[6,2,256,256]{3,2,1,0:T(8,128)(2,1)} %bitcast.5, bf16[8,256,256]{2,1,0:T(8,128)(2,1)} %bitcast.6, s32[8,128]{1,0:T(8,128)} %copy-done.5, s32[8,128]{1,0:T(8,128)} %scatter.14.mc_ref), custom_call_target="tpu_custom_call" | custom-call | tf_op jit(solution)/shard_map/gather_blocks/pallas_call | solution.py:263
  131.6 0.0 copy-start.1
  131.6 2.2 %copy-done.1 = bf16[4,8,256,256]{3,2,1,0:T(8,128)(2,1)S(1)} copy-done((bf16[4,8,256,256]{3,2,1,0:T(8,128)(2,1)S(1)}, bf16[4,8,256,256]{3,2,1,0:T(8,128)(2,1)}, u32[]{:S(2)}) %copy-start.1) | copy-done | bytes 4194328
  133.8 0.0 copy-start.2
  133.8 0.8 copy-done.2
  134.6 0.0 copy-start.3
  134.6 0.7 copy-done.3
  135.3 0.0 copy-start.4
  135.3 0.7 copy-done.4
  135.9 25.0 %block_products.1 = (f32[2,8,256,256]{3,2,1,0:T(8,128)S(1)}, f32[2,8,256]{2,1,0:T(8,128)S(1)}) custom-call(s32[8,8,128]{2,1,0:T(8,128)S(1)} %copy-done.2, s32[4,8,128]{2,1,0:T(8,128)S(1)} %copy-done.3, s32[2]{0:T(128)S(1)} %copy-done.4, bf16[8,12,256,256]{3,2,1,0:T(8,128)(2,1)} %bitcast.4, bf16[4,8,256,256]{3,2,1,0:T(8,128)(2,1)S(1)} %copy-done.1), custom_call_target="tpu_custom_call" | custom-call | tf_op jit(solution)/shard_map/block_products/pallas_call | solution.py:283
  160.9 0.0 copy-start
  160.9 1.9 %copy-done = f32[2,8,256,256]{3,2,1,0:T(8,128)} copy-done((f32[2,8,256,256]{3,2,1,0:T(8,128)}, f32[2,8,256,256]{3,2,1,0:T(8,128)S(1)}, u32[]{:S(2)}) %copy-start) | copy-done | bytes 4194328
  162.9 8.4 %psum.7 = f32[2,256]{1,0:T(2,128)S(1)} all-reduce(f32[2,256]{1,0:T(2,128)S(1)} %reduce_sum.9), channel_id=1, replica_groups=mesh['row'=8,'col'=4] {'col'}, use_global_device_ids=true, to_apply=%region_1.0 | all-reduce | flops 512 | bytes 4096 | tf_op jit(solution)/shard_map/psum | solution.py:306
  171.3 3.9 %multiply_convert_fusion = bf16[2,8,256,256]{3,2,1,0:T(8,128)(2,1)} fusion(f32[2,8,256,256]{3,2,1,0:T(8,128)} %copy-done, f32[2,256]{1,0:T(2,128)S(1)} %broadcast_divide_fusion), kind=kLoop, calls=%fused_computation | loop fusion | flops 2097152 | bytes 6293504 | tf_op jit(solution)/shard_map/convert_element_type | solution.py:308
  (3 shorter events, 0.0 us)
Async XLA Ops:
  2.9 0.6 copy-start.5
  131.6 2.2 %copy-start.1 = (bf16[4,8,256,256]{3,2,1,0:T(8,128)(2,1)S(1)}, bf16[4,8,256,256]{3,2,1,0:T(8,128)(2,1)}, u32[]{:S(2)}) copy-start(bf16[4,8,256,256]{3,2,1,0:T(8,128)(2,1)} %get-tuple-element.50.b_ref) | copy-start | bytes 12582916
  133.8 0.8 copy-start.2
  134.6 0.7 copy-start.3
  135.3 0.7 copy-start.4
  160.9 1.9 %copy-start = (f32[2,8,256,256]{3,2,1,0:T(8,128)}, f32[2,8,256,256]{3,2,1,0:T(8,128)S(1)}, u32[]{:S(2)}) copy-start(f32[2,8,256,256]{3,2,1,0:T(8,128)S(1)} %get-tuple-element.51) | copy-start | bytes 12582916

commit v2 on v1

v2 whole, which is shorter than its diff:
```python
import functools

import jax
import jax.numpy as jnp
from jax import lax
from jax.experimental import pallas as pl
from jax.experimental.pallas import tpu as pltpu
from jax.sharding import PartitionSpec as P

RB_DEV = 8
MESH = pl.DeviceIdType.MESH
CHUNKS = 6
PLAIN = CHUNKS - 1
UP, DOWN, SIDE = 0, 1, 2


def step_kernel(n_row, n_col, shape, a_ref, b_ref, rows_ref, counts_ref, inner_ref, slab_counts, out_ref,
                a_all, b_all, rows_all, counts_all, inner_all, rows_s, counts_s, inner_s,
                stage, dense, right, acc, sums_all,
                send, recv, b_send, b_recv, m_send, m_recv, s_send, s_recv, local):
    columns, slots, per_rank, capacity, block = shape
    n_z = n_row // 2
    r = lax.axis_index("row")
    c = lax.axis_index("col")
    z = lax.div(r, 2)
    y = lax.rem(r, 2)
    other = 1 - y
    beside = 2 * z + other
    has_up = z < n_z - 1
    has_down = z > 0

    barrier = pltpu.get_barrier_semaphore()
    for d in range(1, n_row):
        pl.semaphore_signal(barrier, inc=1, device_id={"row": lax.rem(r + d, n_row)}, device_id_type=MESH)
    for d in range(1, n_col):
        pl.semaphore_signal(barrier, inc=1, device_id={"col": lax.rem(c + d, n_col)}, device_id_type=MESH)
    pl.semaphore_wait(barrier, n_row + n_col - 2)

    def chunk(way, rank, ch, own=False):
        target = {UP: r + 2, DOWN: r - 2, SIDE: beside}[way]
        src = a_ref.at[ch] if own else a_all.at[rank, ch]
        return pltpu.make_async_remote_copy(
            src_ref=src, dst_ref=a_all.at[rank, ch], send_sem=send.at[way, rank, ch],
            recv_sem=recv.at[rank, ch], device_id={"row": target}, device_id_type=MESH)

    def arrived(rank, ch):
        pltpu.make_async_remote_copy(
            src_ref=a_all.at[rank, ch], dst_ref=a_all.at[rank, ch], send_sem=send.at[SIDE, rank, ch],
            recv_sem=recv.at[rank, ch], device_id={"row": beside}, device_id_type=MESH).wait_recv()

    def small(d):
        target = {"row": lax.rem(r + d, n_row)}
        return [
            pltpu.make_async_remote_copy(
                src_ref=src, dst_ref=dst.at[r], send_sem=m_send.at[n, d], recv_sem=m_recv.at[n, d],
                device_id=target, device_id_type=MESH)
            for n, (src, dst) in enumerate(((rows_ref, rows_all), (counts_ref, counts_all)))
        ]

    def slab(d):
        target = {"col": lax.rem(c + d, n_col)}
        return [
            pltpu.make_async_remote_copy(
                src_ref=inner_ref, dst_ref=inner_all.at[c], send_sem=b_send.at[1, d], recv_sem=b_recv.at[1, d],
                device_id=target, device_id_type=MESH),
            pltpu.make_async_remote_copy(
                src_ref=b_ref, dst_ref=b_all.at[c], send_sem=b_send.at[0, d], recv_sem=b_recv.at[0, d],
                device_id=target, device_id_type=MESH),
        ]

    def share(d):
        return pltpu.make_async_remote_copy(
            src_ref=sums_all.at[c], dst_ref=sums_all.at[c], send_sem=s_send.at[d], recv_sem=s_recv.at[d],
            device_id={"col": lax.rem(c + d, n_col)}, device_id_type=MESH)

    for ch in [PLAIN] + list(range(PLAIN)):
        chunk(SIDE, r, ch, True).start()
    for ch in range(CHUNKS):
        @pl.when(has_up)
        def _():
            chunk(UP, r, ch, True).start()

        @pl.when(has_down)
        def _():
            chunk(DOWN, r, ch, True).start()

    for d in range(1, n_row):
        for copy in small(d):
            copy.start()
    for d in range(1, n_col):
        for copy in slab(d):
            copy.start()
    mine = (
        pltpu.make_async_copy(a_ref, a_all.at[r], local.at[0]),
        pltpu.make_async_copy(b_ref, b_all.at[c], local.at[1]),
    )
    for copy in mine:
        copy.start()
    rows_all[r] = rows_ref[...]
    counts_all[r] = counts_ref[...]
    inner_all[c] = inner_ref[...]
    acc[...] = jnp.zeros_like(acc)

    arrived(beside, PLAIN)

    @pl.when(has_up)
    def _():
        chunk(UP, beside, PLAIN).start()

    @pl.when(has_down)
    def _():
        chunk(DOWN, beside, PLAIN).start()

    steps = [(0, ch, True) for ch in range(PLAIN)] + [(0, PLAIN, False), (1, PLAIN, False)]

    def relay(d):
        for flip, ch, cross in steps:
            column = other if flip else y

            @pl.when(z >= d)
            def _():
                rank = 2 * (z - d) + column
                arrived(rank, ch)

                @pl.when(has_up)
                def _():
                    chunk(UP, rank, ch).start()

                if cross:
                    chunk(SIDE, rank, ch).start()

            @pl.when(z + d < n_z)
            def _():
                rank = 2 * (z + d) + column
                arrived(rank, ch)

                @pl.when(has_down)
                def _():
                    chunk(DOWN, rank, ch).start()

                if cross:
                    chunk(SIDE, rank, ch).start()

    def multiply(rank):
        copy = pltpu.make_async_copy(a_all.at[rank], stage, local.at[2])
        copy.start()
        for kk in range(per_rank):
            k = rank * per_rank + kk
            for j in range(columns):
                q = jnp.int32(-1)
                for s in range(n_col * slots):
                    found = (inner_s[s // slots, j, s % slots] == k) & (s < slab_counts[j])
                    q = jnp.where(found, s, q)
                at = jnp.maximum(q, 0)
                value = b_all[lax.div(at, slots), j * slots + lax.rem(at, slots)]
                right[pl.ds(kk * block, block), pl.ds(j * block, block)] = jnp.where(q >= 0, value, jnp.zeros_like(value))
        copy.wait()

        def block_row(i, carry):
            for kk in range(per_rank):
                t = jnp.int32(-1)
                for s in range(capacity):
                    found = (rows_s[rank, kk, s] == i) & (s < counts_s[rank, kk, 0])
                    t = jnp.where(found, s, t)
                at = jnp.maximum(t, 0) + kk * capacity
                size = stage.shape[1]
                value = stage[lax.div(at, size), lax.rem(at, size)]
                dense[:, pl.ds(kk * block, block)] = jnp.where(t >= 0, value, jnp.zeros_like(value))
            rows = pl.ds(pl.multiple_of(i * block, block), block)
            acc[rows, :] += jnp.dot(dense[...], right[...], preferred_element_type=jnp.float32)
            return carry

        lax.fori_loop(0, RB_DEV, block_row, 0)

    def both(d, column, crossed):
        @pl.when(z >= d)
        def _():
            rank = 2 * (z - d) + column
            if crossed:
                for ch in range(PLAIN):
                    arrived(rank, ch)
            multiply(rank)

        @pl.when(z + d < n_z)
        def _():
            rank = 2 * (z + d) + column
            if crossed:
                for ch in range(PLAIN):
                    arrived(rank, ch)
            multiply(rank)

    relay(1)
    for copy in mine:
        copy.wait()
    for d in range(1, n_row):
        for copy in small(d):
            copy.wait()
    for d in range(1, n_col):
        for copy in slab(d):
            copy.wait()
    for n, (src, dst) in enumerate(((rows_all, rows_s), (counts_all, counts_s), (inner_all, inner_s))):
        copy = pltpu.make_async_copy(src, dst, local.at[3 + n])
        copy.start()
        copy.wait()

    multiply(r)
    for ch in range(PLAIN):
        arrived(beside, ch)
    multiply(beside)

    def later(d, carry):
        relay(d)
        both(d - 1, y, False)
        both(d - 1, other, True)
        return carry

    lax.fori_loop(2, n_z, later, 0)
    both(n_z - 1, y, False)
    both(n_z - 1, other, True)

    def square(i, total):
        rows = pl.ds(pl.multiple_of(i * block, block), block)
        value = acc[rows, :]
        value = value * value
        acc[rows, :] = value
        return total + jnp.sum(value.reshape(block // 8, 8, columns * block), axis=0)

    total = lax.fori_loop(0, RB_DEV, square, jnp.zeros((8, columns * block), jnp.float32))
    sums_all[c] = total
    for d in range(1, n_col):
        share(d).start()

    for ch in range(CHUNKS):
        chunk(SIDE, r, ch, True).wait_send()

        @pl.when(has_up)
        def _():
            chunk(UP, r, ch, True).wait_send()

        @pl.when(has_down)
        def _():
            chunk(DOWN, r, ch, True).wait_send()

    @pl.when(has_up)
    def _():
        chunk(UP, beside, PLAIN).wait_send()

    @pl.when(has_down)
    def _():
        chunk(DOWN, beside, PLAIN).wait_send()

    def drain(d, carry):
        for flip, ch, cross in steps:
            column = other if flip else y

            @pl.when(z >= d)
            def _():
                rank = 2 * (z - d) + column

                @pl.when(has_up)
                def _():
                    chunk(UP, rank, ch).wait_send()

                if cross:
                    chunk(SIDE, rank, ch).wait_send()

            @pl.when(z + d < n_z)
            def _():
                rank = 2 * (z + d) + column

                @pl.when(has_down)
                def _():
                    chunk(DOWN, rank, ch).wait_send()

                if cross:
                    chunk(SIDE, rank, ch).wait_send()
        return carry

    lax.fori_loop(1, n_z, drain, 0)

    for d in range(1, n_col):
        share(d).wait()
    sums = jnp.sum(jnp.sum(sums_all[...], axis=0), axis=0, keepdims=True)
    factor = float(RB_DEV * n_col * block) / sums

    def scale(i, carry):
        rows = pl.ds(pl.multiple_of(i * block, block), block)
        value = (acc[rows, :] * factor).astype(jnp.bfloat16)
        for j in range(columns):
            out_ref[j, i] = value[:, j * block:(j + 1) * block]
        return carry

    lax.fori_loop(0, RB_DEV, scale, 0)


def on_device(n_row, n_col, matrix_blocks, matrix_rows, matrix_counts, slab_blocks, slab_inner, slab_counts):
    per_rank, capacity, block = matrix_blocks.shape[0], matrix_blocks.shape[1], matrix_blocks.shape[2]
    columns, slots = slab_blocks.shape[0], slab_blocks.shape[1]
    held = per_rank * capacity
    size = held // CHUNKS
    a = matrix_blocks.reshape(CHUNKS, size, block, block)
    b = slab_blocks.reshape(columns * slots, block, block)
    hbm = pl.BlockSpec(memory_space=pl.ANY)
    vmem = pl.BlockSpec(memory_space=pltpu.VMEM)
    dma = pltpu.SemaphoreType.DMA
    rows_shape, counts_shape, inner_shape = (
        (n_row,) + matrix_rows.shape, (n_row,) + matrix_counts.shape, (n_col,) + slab_inner.shape)
    return pl.pallas_call(
        functools.partial(step_kernel, n_row, n_col, (columns, slots, per_rank, capacity, block)),
        out_shape=jax.ShapeDtypeStruct((columns, RB_DEV, block, block), jnp.bfloat16),
        in_specs=[hbm, hbm, vmem, vmem, vmem, pl.BlockSpec(memory_space=pltpu.SMEM)],
        out_specs=vmem,
        scratch_shapes=[
            pltpu.VMEM((n_row,) + a.shape, a.dtype),
            pltpu.VMEM((n_col,) + b.shape, b.dtype),
            pltpu.VMEM(rows_shape, jnp.int32),
            pltpu.VMEM(counts_shape, jnp.int32),
            pltpu.VMEM(inner_shape, jnp.int32),
            pltpu.SMEM(rows_shape, jnp.int32),
            pltpu.SMEM(counts_shape, jnp.int32),
            pltpu.SMEM(inner_shape, jnp.int32),
            pltpu.VMEM(a.shape, a.dtype),
            pltpu.VMEM((block, per_rank * block), a.dtype),
            pltpu.VMEM((per_rank * block, columns * block), b.dtype),
            pltpu.VMEM((RB_DEV * block, columns * block), jnp.float32),
            pltpu.VMEM((n_col, 8, columns * block), jnp.float32),
            dma((3, n_row, CHUNKS)), dma((n_row, CHUNKS)),
            dma((2, n_col)), dma((2, n_col)), dma((2, n_row)), dma((2, n_row)), dma((n_col,)), dma((n_col,)),
            dma((6,)),
        ],
        compiler_params=pltpu.CompilerParams(
            collective_id=0, has_side_effects=True, vmem_limit_bytes=52 << 20),
        name="gather_multiply_normalize",
    )(a, b, matrix_rows, matrix_counts, slab_inner, slab_counts)


def solution(mesh):
    return jax.shard_map(
        functools.partial(on_device, mesh.shape["row"], mesh.shape["col"]),
        mesh=mesh,
        in_specs=(
            P("row", "col", None, None),
            P("row", "col"),
            P("row", "col"),
            P("row", "col", None, None),
            P("row", "col"),
            P("row"),
        ),
        out_specs=P("row", "col", None, None),
        check_vma=False,
    )
```

time: 175 us -> 151 us (0.86)
  Pallas kernels: 153 us -> 144 us
  blocking collectives: 8.38 us -> 0 us
  other arithmetic: 3.97 us -> 0 us
  local copies, waits for them, and re-layouts: 9.69 us -> 7.07 us
    pallas_call x2 -> x1, Pallas kernels: 153 us -> 144 us  [on_device(): pl.pallas_call(functools.partial(step_kernel, n_row, n_col, (columns, slo...]
    psum x1 -> x0, blocking collectives: 8.38 us -> none  [on_device(): sums = lax.psum(jnp.sum(partial, axis=1), 'col')]
    convert_element_type x1 -> x0, other arithmetic: 3.94 us -> none  [on_device(): return (squared * factor[:, None, None, :]).astype(jnp.bfloat16)]
    unnamed x12 -> x10, local copies, waits for them, and re-layouts: 6.82 us -> 7.07 us
where the time goes in v2:
time: 151 us
  Pallas kernels  144 us (95%)
  local copies, waits for them, and re-layouts  7.07 us (5%)
    pallas_call x1, Pallas kernels, on_device(): pl.pallas_call(functools.partial(step_kernel, n_row, n_col, (columns, slo...  144 us
    unnamed x10, local copies, waits for them, and re-layouts  7.07 us

profile of v2, /device:TPU:0, one launch (start us, length us, event | category | flops | bytes accessed | tf_op | source)
XLA Modules:
  0.0 151.2 jit_solution(7550216651601413968)
XLA Ops:
  0.0 0.7 copy.7.counts_ref
  0.7 0.0 copy-start
  0.7 1.2 copy-done
  2.0 0.0 copy-start.1
  2.0 0.7 copy-done.1
  2.6 0.0 copy-start.2
  2.6 0.7 copy-done.2
  3.3 0.0 copy-start.3
  3.3 0.7 copy-done.3
  4.0 144.2 %gather_multiply_normalize.1 = bf16[2,8,256,256]{3,2,1,0:T(8,128)(2,1)} custom-call(bf16[6,2,256,256]{3,2,1,0:T(8,128)(2,1)} %bitcast.3, bf16[8,256,256]{2,1,0:T(8,128)(2,1)S(1)} %bitcast.2, s32[2,6]{1,0:T(2,128)S(1)} %copy-done.1, s32[2,1]{1,0:T(2,128)S(1)} %copy.7.counts_ref, s32[2,4]{1,0:T(2,128)S(1)} %copy-done.2, s32[2]{0:T(128)S(1)} %copy-done.3), custom_call_target="tpu_custom_call" | custom-call | tf_op jit(solution)/shard_map/gather_multiply_normalize/pallas_call | solution.py:308
  148.1 3.1 %copy.9 = bf16[2,8,256,256]{3,2,1,0:T(8,128)(2,1)} copy(bf16[2,8,256,256]{3,2,1,0:T(8,128)(2,1)} %gather_multiply_normalize.1) | data formatting | bytes 4194304
Async XLA Ops:
  0.7 1.2 copy-start
  2.0 0.7 copy-start.1
  2.6 0.7 copy-start.2
  3.3 0.7 copy-start.3

commit v3 on v2

--- a/solution.py
+++ b/solution.py
@@ -16,9 +16,11 @@
 
 def step_kernel(n_row, n_col, shape, a_ref, b_ref, rows_ref, counts_ref, inner_ref, slab_counts, out_ref,
                 a_all, b_all, rows_all, counts_all, inner_all, rows_s, counts_s, inner_s,
-                stage, dense, right, acc, sums_all,
+                slot_s, source_s, stage, right, acc, sums_all,
                 send, recv, b_send, b_recv, m_send, m_recv, s_send, s_recv, local):
     columns, slots, per_rank, capacity, block = shape
+    each = CHUNKS // per_rank
+    size = capacity // each
     n_z = n_row // 2
     r = lax.axis_index("row")
     c = lax.axis_index("col")
@@ -93,12 +95,12 @@
     mine = (
         pltpu.make_async_copy(a_ref, a_all.at[r], local.at[0]),
         pltpu.make_async_copy(b_ref, b_all.at[c], local.at[1]),
+        pltpu.make_async_copy(rows_ref, rows_all.at[r], local.at[2]),
+        pltpu.make_async_copy(counts_ref, counts_all.at[r], local.at[3]),
+        pltpu.make_async_copy(inner_ref, inner_all.at[c], local.at[4]),
     )
     for copy in mine:
         copy.start()
-    rows_all[r] = rows_ref[...]
-    counts_all[r] = counts_ref[...]
-    inner_all[c] = inner_ref[...]
     acc[...] = jnp.zeros_like(acc)
 
     arrived(beside, PLAIN)
@@ -113,8 +115,19 @@
 
     steps = [(0, ch, True) for ch in range(PLAIN)] + [(0, PLAIN, False), (1, PLAIN, False)]
 
-    def relay(d):
-        for flip, ch, cross in steps:
+    def sides(d, work):
+        def one(side, carry):
+            at = z + d * (2 * side - 1)
+
+            @pl.when((at >= 0) & (at < n_z))
+            def _():
+                work(at)
+            return carry
+
+        lax.fori_loop(0, 2, one, 0)
+
+    def relay(d, extra):
+        for n, (flip, ch, cross) in enumerate(steps):
             column = other if flip else y
 
             @pl.when(z >= d)
@@ -141,55 +154,61 @@
                 if cross:
                     chunk(SIDE, rank, ch).start()
 
-    def multiply(rank):
-        copy = pltpu.make_async_copy(a_all.at[rank], stage, local.at[2])
+            for work in extra.get(n, ()):
+                work()
+
+    def half(rank, kk):
+        k = rank * per_rank + kk
+        copy = pltpu.make_async_copy(a_all.at[rank, pl.ds(kk * each, each)], stage, local.at[0])
         copy.start()
-        for kk in range(per_rank):
-            k = rank * per_rank + kk
-            for j in range(columns):
-                q = jnp.int32(-1)
-                for s in range(n_col * slots):
-                    found = (inner_s[s // slots, j, s % slots] == k) & (s < slab_counts[j])
-                    q = jnp.where(found, s, q)
-                at = jnp.maximum(q, 0)
-                value = b_all[lax.div(at, slots), j * slots + lax.rem(at, slots)]
-                right[pl.ds(kk * block, block), pl.ds(j * block, block)] = jnp.where(q >= 0, value, jnp.zeros_like(value))
+        for j in range(columns):
+            q = source_s[k, j]
+            at = jnp.maximum(q, 0)
+            value = b_all[lax.div(at, slots), j * slots + lax.rem(at, slots)]
+            right[:, j * block:(j + 1) * block] = jnp.where(q >= 0, value, jnp.zeros_like(value))
         copy.wait()
 
         def block_row(i, carry):
-            for kk in range(per_rank):
-                t = jnp.int32(-1)
-                for s in range(capacity):
-                    found = (rows_s[rank, kk, s] == i) & (s < counts_s[rank, kk, 0])
-                    t = jnp.where(found, s, t)
-                at = jnp.maximum(t, 0) + kk * capacity
-                size = stage.shape[1]
-                value = stage[lax.div(at, size), lax.rem(at, size)]
-                dense[:, pl.ds(kk * block, block)] = jnp.where(t >= 0, value, jnp.zeros_like(value))
+            t = slot_s[k, i]
+            at = jnp.maximum(t, 0)
+            value = stage[lax.div(at, size), lax.rem(at, size)]
+            left = jnp.where(t >= 0, value, jnp.zeros_like(value))
             rows = pl.ds(pl.multiple_of(i * block, block), block)
-            acc[rows, :] += jnp.dot(dense[...], right[...], preferred_element_type=jnp.float32)
+            acc[rows, :] += jnp.dot(left, right[...], preferred_element_type=jnp.float32)
             return carry
 
-        lax.fori_loop(0, RB_DEV, block_row, 0)
-
-    def both(d, column, crossed):
-        @pl.when(z >= d)
-        def _():
-            rank = 2 * (z - d) + column
-            if crossed:
-                for ch in range(PLAIN):
-                    arrived(rank, ch)
-            multiply(rank)
-
-        @pl.when(z + d < n_z)
-        def _():
-            rank = 2 * (z + d) + column
-            if crossed:
-                for ch in range(PLAIN):
-                    arrived(rank, ch)
-            multiply(rank)
-
-    relay(1)
+        lax.fori_loop(0, RB_DEV, block_row, 0, unroll=2)
+
+    def whole(rank):
+        def one(kk, carry):
+            half(rank, kk)
+            return carry
+
+        lax.fori_loop(0, per_rank, one, 0)
+
+    def await_side(rank, first, end):
+        for ch in range(first, end):
+            arrived(rank, ch)
+
+    def own_whole(at):
+        whole(2 * at + y)
+
+    def side_whole(at):
+        await_side(2 * at + other, 0, PLAIN)
+        whole(2 * at + other)
+
+    def own_half(kk):
+        def work(at):
+            half(2 * at + y, kk)
+        return work
+
+    def side_half(kk):
+        def work(at):
+            await_side(2 * at + other, kk * each, min(kk * each + each, PLAIN))
+            half(2 * at + other, kk)
+        return work
+
+    relay(1, {})
     for copy in mine:
         copy.wait()
     for d in range(1, n_row):
@@ -199,30 +218,55 @@
         for copy in slab(d):
             copy.wait()
     for n, (src, dst) in enumerate(((rows_all, rows_s), (counts_all, counts_s), (inner_all, inner_s))):
-        copy = pltpu.make_async_copy(src, dst, local.at[3 + n])
+        copy = pltpu.make_async_copy(src, dst, local.at[5 + n])
         copy.start()
         copy.wait()
 
-    multiply(r)
-    for ch in range(PLAIN):
-        arrived(beside, ch)
-    multiply(beside)
+    def table(rank, carry):
+        for kk in range(per_rank):
+            k = rank * per_rank + kk
+            for j in range(columns):
+                q = jnp.int32(-1)
+                for n in range(n_col * slots):
+                    found = (inner_s[n // slots, j, n % slots] == k) & (n < slab_counts[j])
+                    q = jnp.where(found, n, q)
+                source_s[k, j] = q
+            for i in range(RB_DEV):
+                t = jnp.int32(-1)
+                for n in range(capacity):
+                    found = (rows_s[rank, kk, n] == i) & (n < counts_s[rank, kk, 0])
+                    t = jnp.where(found, n, t)
+                slot_s[k, i] = t
+        return carry
+
+    lax.fori_loop(0, n_row, table, 0)
+    await_side(beside, 0, PLAIN)
+
+    def here(column, carry):
+        whole(2 * z + column)
+        return carry
+
+    lax.fori_loop(0, 2, here, 0)
+    sides(1, own_whole)
 
     def later(d, carry):
-        relay(d)
-        both(d - 1, y, False)
-        both(d - 1, other, True)
-        return carry
-
-    lax.fori_loop(2, n_z, later, 0)
-    both(n_z - 1, y, False)
-    both(n_z - 1, other, True)
+        relay(d, {})
+        sides(d - 1, side_whole)
+        sides(d, own_whole)
+        return carry
+
+    lax.fori_loop(2, n_z - 1, later, 0)
+    far = n_z - 1
+    relay(far, {
+        each - 1: (lambda: sides(far, own_half(0)), lambda: sides(far - 1, side_whole)),
+        CHUNKS - 1: (lambda: sides(far, own_half(1)), lambda: sides(far, side_half(0))),
+        CHUNKS: (lambda: sides(far, side_half(1)),),
+    })
 
     def square(i, total):
         rows = pl.ds(pl.multiple_of(i * block, block), block)
         value = acc[rows, :]
         value = value * value
-        acc[rows, :] = value
         return total + jnp.sum(value.reshape(block // 8, 8, columns * block), axis=0)
 
     total = lax.fori_loop(0, RB_DEV, square, jnp.zeros((8, columns * block), jnp.float32))
@@ -285,7 +329,8 @@
 
     def scale(i, carry):
         rows = pl.ds(pl.multiple_of(i * block, block), block)
-        value = (acc[rows, :] * factor).astype(jnp.bfloat16)
+        value = acc[rows, :]
+        value = (value * value * factor).astype(jnp.bfloat16)
         for j in range(columns):
             out_ref[j, i] = value[:, j * block:(j + 1) * block]
         return carry
@@ -300,7 +345,7 @@
     size = held // CHUNKS
     a = matrix_blocks.reshape(CHUNKS, size, block, block)
     b = slab_blocks.reshape(columns * slots, block, block)
-    hbm = pl.BlockSpec(memory_space=pl.ANY)
+    hbm = pl.BlockSpec(memory_space=pltpu.HBM)
     vmem = pl.BlockSpec(memory_space=pltpu.VMEM)
     dma = pltpu.SemaphoreType.DMA
     rows_shape, counts_shape, inner_shape = (
@@ -308,7 +353,7 @@
     return pl.pallas_call(
         functools.partial(step_kernel, n_row, n_col, (columns, slots, per_rank, capacity, block)),
         out_shape=jax.ShapeDtypeStruct((columns, RB_DEV, block, block), jnp.bfloat16),
-        in_specs=[hbm, hbm, vmem, vmem, vmem, pl.BlockSpec(memory_space=pltpu.SMEM)],
+        in_specs=[hbm, hbm, hbm, hbm, hbm, pl.BlockSpec(memory_space=pltpu.SMEM)],
         out_specs=vmem,
         scratch_shapes=[
             pltpu.VMEM((n_row,) + a.shape, a.dtype),
@@ -319,17 +364,18 @@
             pltpu.SMEM(rows_shape, jnp.int32),
             pltpu.SMEM(counts_shape, jnp.int32),
             pltpu.SMEM(inner_shape, jnp.int32),
-            pltpu.VMEM(a.shape, a.dtype),
-            pltpu.VMEM((block, per_rank * block), a.dtype),
-            pltpu.VMEM((per_rank * block, columns * block), b.dtype),
+            pltpu.SMEM((n_row * per_rank, RB_DEV), jnp.int32),
+            pltpu.SMEM((n_row * per_rank, columns), jnp.int32),
+            pltpu.VMEM((CHUNKS // per_rank, size, block, block), a.dtype),
+            pltpu.VMEM((block, columns * block), b.dtype),
             pltpu.VMEM((RB_DEV * block, columns * block), jnp.float32),
             pltpu.VMEM((n_col, 8, columns * block), jnp.float32),
             dma((3, n_row, CHUNKS)), dma((n_row, CHUNKS)),
             dma((2, n_col)), dma((2, n_col)), dma((2, n_row)), dma((2, n_row)), dma((n_col,)), dma((n_col,)),
-            dma((6,)),
+            dma((8,)),
         ],
         compiler_params=pltpu.CompilerParams(
-            collective_id=0, has_side_effects=True, vmem_limit_bytes=52 << 20),
+            collective_id=0, has_side_effects=True, vmem_limit_bytes=63 << 20),
         name="gather_multiply_normalize",
     )(a, b, matrix_rows, matrix_counts, slab_inner, slab_counts)
 

time: 151 us -> 140 us (0.927)
  Pallas kernels: 144 us -> 135 us
  local copies, waits for them, and re-layouts: 7.07 us -> 4.39 us
    pallas_call x1, Pallas kernels: 144 us -> 135 us  [on_device(): pl.pallas_call(functools.partial(step_kernel, n_row, n_col, (columns, slo...]
    unnamed x10 -> x2, local copies, waits for them, and re-layouts: 7.07 us -> 4.39 us
where the time goes in v3:
time: 140 us
  Pallas kernels  135 us (96%)
  local copies, waits for them, and re-layouts  4.39 us (3%)
    pallas_call x1, Pallas kernels, on_device(): pl.pallas_call(functools.partial(step_kernel, n_row, n_col, (columns, slo...  135 us
    unnamed x2, local copies, waits for them, and re-layouts  4.39 us

profile of v3, /device:TPU:0, one launch (start us, length us, event | category | flops | bytes accessed | tf_op | source)
XLA Modules:
  0.0 139.6 jit_solution(17324554674440661432)
XLA Ops:
  0.0 1.3 copy.7.counts_ref
  1.3 135.2 %gather_multiply_normalize.1 = bf16[2,8,256,256]{3,2,1,0:T(8,128)(2,1)} custom-call(bf16[6,2,256,256]{3,2,1,0:T(8,128)(2,1)} %bitcast.2, bf16[8,256,256]{2,1,0:T(8,128)(2,1)} %bitcast.3, s32[2,6]{1,0:T(2,128)} %rows_ref.1, s32[2,1]{1,0:T(2,128)} %copy.7.counts_ref, s32[2,4]{1,0:T(2,128)} %inner_ref.1, s32[2]{0:T(128)} %slab_counts.1), custom_call_target="tpu_custom_call" | custom-call | tf_op jit(solution)/shard_map/gather_multiply_normalize/pallas_call | solution.py:353
  136.5 3.1 %copy.9 = bf16[2,8,256,256]{3,2,1,0:T(8,128)(2,1)} copy(bf16[2,8,256,256]{3,2,1,0:T(8,128)(2,1)} %gather_multiply_normalize.1) | data formatting | bytes 4194304

commit v4 on v3

--- a/solution.py
+++ b/solution.py
@@ -16,8 +16,8 @@
 
 def step_kernel(n_row, n_col, shape, a_ref, b_ref, rows_ref, counts_ref, inner_ref, slab_counts, out_ref,
                 a_all, b_all, rows_all, counts_all, inner_all, rows_s, counts_s, inner_s,
-                slot_s, source_s, stage, right, acc, sums_all,
-                send, recv, b_send, b_recv, m_send, m_recv, s_send, s_recv, local):
+                slot_s, source_s, stage, right, acc, sums_all, result,
+                send, recv, b_send, b_recv, m_send, m_recv, s_send, s_recv, local, done):
     columns, slots, per_rank, capacity, block = shape
     each = CHUNKS // per_rank
     size = capacity // each
@@ -234,7 +234,7 @@
             for i in range(RB_DEV):
                 t = jnp.int32(-1)
                 for n in range(capacity):
-                    found = (rows_s[rank, kk, n] == i) & (n < counts_s[rank, kk, 0])
+                    found = (rows_s[rank, kk, n] == i) & (n < counts_s[rank, 0, kk])
                     t = jnp.where(found, n, t)
                 slot_s[k, i] = t
         return carry
@@ -257,8 +257,13 @@
 
     lax.fori_loop(2, n_z - 1, later, 0)
     far = n_z - 1
+
+    def side_halves(at):
+        side_half(0)(at)
+        side_half(1)(at)
+
     relay(far, {
-        each - 1: (lambda: sides(far, own_half(0)), lambda: sides(far - 1, side_whole)),
+        each - 1: (lambda: sides(far, own_half(0)), lambda: sides(far - 1, side_halves)),
         CHUNKS - 1: (lambda: sides(far, own_half(1)), lambda: sides(far, side_half(0))),
         CHUNKS: (lambda: sides(far, side_half(1)),),
     })
@@ -332,10 +337,18 @@
         value = acc[rows, :]
         value = (value * value * factor).astype(jnp.bfloat16)
         for j in range(columns):
-            out_ref[j, i] = value[:, j * block:(j + 1) * block]
+            result[j, i] = value[:, j * block:(j + 1) * block]
+            pltpu.make_async_copy(result.at[j, i], out_ref.at[j, i], done.at[j, i]).start()
         return carry
 
     lax.fori_loop(0, RB_DEV, scale, 0)
+
+    def finish(i, carry):
+        for j in range(columns):
+            pltpu.make_async_copy(result.at[j, i], out_ref.at[j, i], done.at[j, i]).wait()
+        return carry
+
+    lax.fori_loop(0, RB_DEV, finish, 0)
 
 
 def on_device(n_row, n_col, matrix_blocks, matrix_rows, matrix_counts, slab_blocks, slab_inner, slab_counts):
@@ -345,8 +358,8 @@
     size = held // CHUNKS
     a = matrix_blocks.reshape(CHUNKS, size, block, block)
     b = slab_blocks.reshape(columns * slots, block, block)
+    matrix_counts = matrix_counts.reshape(1, per_rank)
     hbm = pl.BlockSpec(memory_space=pltpu.HBM)
-    vmem = pl.BlockSpec(memory_space=pltpu.VMEM)
     dma = pltpu.SemaphoreType.DMA
     rows_shape, counts_shape, inner_shape = (
         (n_row,) + matrix_rows.shape, (n_row,) + matrix_counts.shape, (n_col,) + slab_inner.shape)
@@ -354,7 +367,7 @@
         functools.partial(step_kernel, n_row, n_col, (columns, slots, per_rank, capacity, block)),
         out_shape=jax.ShapeDtypeStruct((columns, RB_DEV, block, block), jnp.bfloat16),
         in_specs=[hbm, hbm, hbm, hbm, hbm, pl.BlockSpec(memory_space=pltpu.SMEM)],
-        out_specs=vmem,
+        out_specs=hbm,
         scratch_shapes=[
             pltpu.VMEM((n_row,) + a.shape, a.dtype),
             pltpu.VMEM((n_col,) + b.shape, b.dtype),
@@ -370,9 +383,10 @@
             pltpu.VMEM((block, columns * block), b.dtype),
             pltpu.VMEM((RB_DEV * block, columns * block), jnp.float32),
             pltpu.VMEM((n_col, 8, columns * block), jnp.float32),
+            pltpu.VMEM((columns, RB_DEV, block, block), jnp.bfloat16),
             dma((3, n_row, CHUNKS)), dma((n_row, CHUNKS)),
             dma((2, n_col)), dma((2, n_col)), dma((2, n_row)), dma((2, n_row)), dma((n_col,)), dma((n_col,)),
-            dma((8,)),
+            dma((8,)), dma((columns, RB_DEV)),
         ],
         compiler_params=pltpu.CompilerParams(
             collective_id=0, has_side_effects=True, vmem_limit_bytes=63 << 20),

time: 140 us -> 138 us (0.986)
    unnamed x2 -> x1, local copies, waits for them, and re-layouts: 4.39 us -> 3.1 us
where the time goes in v4:
time: 138 us
  Pallas kernels  135 us (98%)
  local copies, waits for them, and re-layouts  3.1 us (2%)
    pallas_call x1, Pallas kernels, on_device(): pl.pallas_call(functools.partial(step_kernel, n_row, n_col, (columns, slo...  135 us
    unnamed x1, local copies, waits for them, and re-layouts  3.1 us

profile of v4, /device:TPU:0, one launch (start us, length us, event | category | flops | bytes accessed | tf_op | source)
XLA Modules:
  0.0 138.0 jit_solution(16624770803311619644)
XLA Ops:
  0.0 134.9 %gather_multiply_normalize.1 = bf16[2,8,256,256]{3,2,1,0:T(8,128)(2,1)} custom-call(bf16[6,2,256,256]{3,2,1,0:T(8,128)(2,1)} %bitcast.3, bf16[8,256,256]{2,1,0:T(8,128)(2,1)} %bitcast.4, s32[2,6]{1,0:T(2,128)} %rows_ref.1, s32[1,2]{1,0:T(1,128)} %bitcast.5, s32[2,4]{1,0:T(2,128)} %inner_ref.1, s32[2]{0:T(128)} %slab_counts.1), custom_call_target="tpu_custom_call" | custom-call | tf_op jit(solution)/shard_map/gather_multiply_normalize/pallas_call | solution.py:366
  134.9 3.1 %copy.8 = bf16[2,8,256,256]{3,2,1,0:T(8,128)(2,1)} copy(bf16[2,8,256,256]{3,2,1,0:T(8,128)(2,1)} %gather_multiply_normalize.1) | data formatting | bytes 4194304

commit v5 on v4

--- a/solution.py
+++ b/solution.py
@@ -209,18 +209,21 @@
         return work
 
     relay(1, {})
-    for copy in mine:
-        copy.wait()
-    for d in range(1, n_row):
-        for copy in small(d):
+
+    def complete():
+        for copy in mine:
             copy.wait()
-    for d in range(1, n_col):
-        for copy in slab(d):
+        for d in range(1, n_row):
+            for copy in small(d):
+                copy.wait()
+        for d in range(1, n_col):
+            for copy in slab(d):
+                copy.wait()
+        for n, (src, dst) in enumerate(((rows_all, rows_s), (counts_all, counts_s), (inner_all, inner_s))):
+            copy = pltpu.make_async_copy(src, dst, local.at[5 + n])
+            copy.start()
             copy.wait()
-    for n, (src, dst) in enumerate(((rows_all, rows_s), (counts_all, counts_s), (inner_all, inner_s))):
-        copy = pltpu.make_async_copy(src, dst, local.at[5 + n])
-        copy.start()
-        copy.wait()
+        lax.fori_loop(0, n_row, table, 0)
 
     def table(rank, carry):
         for kk in range(per_rank):
@@ -239,15 +242,18 @@
                 slot_s[k, i] = t
         return carry
 
-    lax.fori_loop(0, n_row, table, 0)
-    await_side(beside, 0, PLAIN)
-
-    def here(column, carry):
-        whole(2 * z + column)
-        return carry
-
-    lax.fori_loop(0, 2, here, 0)
-    sides(1, own_whole)
+    def side_here():
+        await_side(beside, 0, PLAIN)
+        whole(beside)
+
+    relay(2, {
+        0: (complete,),
+        1: (lambda: whole(r),),
+        2: (side_here,),
+        3: (lambda: sides(1, own_whole),),
+    })
+    sides(1, side_whole)
+    sides(2, own_whole)
 
     def later(d, carry):
         relay(d, {})
@@ -255,7 +261,7 @@
         sides(d, own_whole)
         return carry
 
-    lax.fori_loop(2, n_z - 1, later, 0)
+    lax.fori_loop(3, n_z - 1, later, 0)
     far = n_z - 1
 
     def side_halves(at):

time: 138 us -> 138 us (level)
  no operation moved by 1% of the time
where the time goes in v5:
time: 138 us
  Pallas kernels  135 us (98%)
  local copies, waits for them, and re-layouts  3.1 us (2%)
    pallas_call x1, Pallas kernels, on_device(): pl.pallas_call(functools.partial(step_kernel, n_row, n_col, (columns, slo...  135 us
    unnamed x1, local copies, waits for them, and re-layouts  3.1 us

profile of v5, /device:TPU:0, one launch (start us, length us, event | category | flops | bytes accessed | tf_op | source)
XLA Modules:
  0.0 138.0 jit_solution(4357825863863450276)
XLA Ops:
  0.0 134.9 %gather_multiply_normalize.1 = bf16[2,8,256,256]{3,2,1,0:T(8,128)(2,1)} custom-call(bf16[6,2,256,256]{3,2,1,0:T(8,128)(2,1)} %bitcast.3, bf16[8,256,256]{2,1,0:T(8,128)(2,1)} %bitcast.4, s32[2,6]{1,0:T(2,128)} %rows_ref.1, s32[1,2]{1,0:T(1,128)} %bitcast.5, s32[2,4]{1,0:T(2,128)} %inner_ref.1, s32[2]{0:T(128)} %slab_counts.1), custom_call_target="tpu_custom_call" | custom-call | tf_op jit(solution)/shard_map/gather_multiply_normalize/pallas_call | solution.py:372
  134.9 3.1 %copy.8 = bf16[2,8,256,256]{3,2,1,0:T(8,128)(2,1)} copy(bf16[2,8,256,256]{3,2,1,0:T(8,128)(2,1)} %gather_multiply_normalize.1) | data formatting | bytes 4194304
